TPU v7x, 32 devices: a whole 2x2x4 slice. The times are simulated.
32 devices in a mesh: dp: 8 (over z, x), ctx: 4 (over y, core).
Axes of the slice: x: 2, y: 2, z: 4, core: 2. Of those that a mesh axis runs over, the one named last changes fastest.
Arguments:
- tokens: bfloat16 [16, 2048, 768], P('dp', 'ctx'), may hold values from -6 to 6
- segments: int32 [16, 2048], P('dp'), may hold values from 0 to 4, never falling along the last dimension, each value on 1 to 800 neighbouring positions
- cotangent: bfloat16 [16, 2048, 768], P('dp', 'ctx'), may hold values from -6 to 6
- query_weight: bfloat16 [768, 768], P(('dp', 'ctx')), may hold values from -0.21875 to 0.21875
- query_bias: bfloat16 [768], P(('dp', 'ctx')), may hold values from -3 to 3
- key_weight: bfloat16 [768, 768], P(('dp', 'ctx')), may hold values from -0.21875 to 0.21875
- value_weight: bfloat16 [768, 768], P(('dp', 'ctx')), may hold values from -0.21875 to 0.21875
- value_bias: bfloat16 [768], P(('dp', 'ctx')), may hold values from -0.59765625 to 0.59765625
- output_weight: bfloat16 [768, 768], P(('dp', 'ctx')), may hold values from -0.875 to 0.875
- output_bias: bfloat16 [768], P(('dp', 'ctx')), may hold values from -2 to 2
- first_gain: bfloat16 [768], P(('dp', 'ctx')), may hold values from 0.5 to 1.5
- first_shift: bfloat16 [768], P(('dp', 'ctx')), may hold values from -2 to 2
- inner_weight: bfloat16 [768, 3072], P(('dp', 'ctx')), may hold values from -0.21875 to 0.21875
- inner_bias: bfloat16 [3072], P(('dp', 'ctx')), may hold values from -3 to 3
- outer_weight: bfloat16 [3072, 768], P(('dp', 'ctx')), may hold values from -0.109375 to 0.109375
- outer_bias: bfloat16 [768], P(('dp', 'ctx')), may hold values from -2 to 2
- second_gain: bfloat16 [768], P(('dp', 'ctx')), may hold values from 0.5 to 1.5
- second_shift: bfloat16 [768], P(('dp', 'ctx')), may hold values from -2 to 2
Outputs:
- layer_output: bfloat16 [16, 2048, 768], P('dp', 'ctx')
- input_gradient: float32 [16, 2048, 768], P('dp', 'ctx')
- query_weight_gradient: float32 [768, 768], P(('dp', 'ctx'))
- query_bias_gradient: float32 [768], P(('dp', 'ctx'))
- key_weight_gradient: float32 [768, 768], P(('dp', 'ctx'))
- value_weight_gradient: float32 [768, 768], P(('dp', 'ctx'))
- value_bias_gradient: float32 [768], P(('dp', 'ctx'))
- output_weight_gradient: float32 [768, 768], P(('dp', 'ctx'))
- output_bias_gradient: float32 [768], P(('dp', 'ctx'))
- first_gain_gradient: float32 [768], P(('dp', 'ctx'))
- first_shift_gradient: float32 [768], P(('dp', 'ctx'))
- inner_weight_gradient: float32 [768, 3072], P(('dp', 'ctx'))
- inner_bias_gradient: float32 [3072], P(('dp', 'ctx'))
- outer_weight_gradient: float32 [3072, 768], P(('dp', 'ctx'))
- outer_bias_gradient: float32 [768], P(('dp', 'ctx'))
- second_gain_gradient: float32 [768], P(('dp', 'ctx'))
- second_shift_gradient: float32 [768], P(('dp', 'ctx'))
Inputs may be any that keep to these rules, and one draw needn't show every extreme that they name: `segments`: in each sequence the document numbers start at 0 and never fall; a document has 1 to 800 tokens, one of each sequence exactly 800, and there are at most 5 documents.
All inputs are finite; a program needn't handle non-finite values.
Results may differ from a plain program's by a relative error of at most 0.028.
Values may be sent and summed in bfloat16 or wider, within the bound.
No kernel may reach another device: no remote copies, remote signals or barrier semaphores. Data moves between devices by JAX's collectives and lax.ppermute only.
A program may use at most 384 MiB of HBM per device.

v0:
```python
import math
import jax
import jax.numpy as jnp
from jax import lax
from jax.sharding import PartitionSpec as P

HEADS = 12
HEAD = 64
epsilon = 1e-05


def layer_norm(values, gain, shift):
    average = jnp.mean(values, axis=-1, keepdims=True)
    centred = values - average
    spread = jnp.mean(centred * centred, axis=-1, keepdims=True)
    return centred * lax.rsqrt(spread + epsilon) * gain + shift


def gelu_exact(values):
    return jax.nn.gelu(values, approximate=False)


def fetch_weights(shards):
    return (
        lax.all_gather(shards[0], ("dp", "ctx"), axis=0, tiled=True),
        lax.all_gather(shards[1], ("dp", "ctx"), axis=0, tiled=True),
        lax.all_gather(shards[2], ("dp", "ctx"), axis=0, tiled=True),
        lax.all_gather(shards[3], ("dp", "ctx"), axis=0, tiled=True),
        lax.all_gather(shards[4], ("dp", "ctx"), axis=0, tiled=True),
        lax.all_gather(shards[5], ("dp", "ctx"), axis=0, tiled=True),
        lax.all_gather(shards[6], ("dp", "ctx"), axis=0, tiled=True),
        lax.all_gather(shards[7], ("dp", "ctx"), axis=0, tiled=True),
        lax.all_gather(shards[8], ("dp", "ctx"), axis=0, tiled=True),
        lax.all_gather(shards[9], ("dp", "ctx"), axis=0, tiled=True),
        lax.all_gather(shards[10], ("dp", "ctx"), axis=0, tiled=True),
        lax.all_gather(shards[11], ("dp", "ctx"), axis=0, tiled=True),
        lax.all_gather(shards[12], ("dp", "ctx"), axis=0, tiled=True),
        lax.all_gather(shards[13], ("dp", "ctx"), axis=0, tiled=True),
        lax.all_gather(shards[14], ("dp", "ctx"), axis=0, tiled=True),
    )


def masked_scores(query_heads, key_heads, allowed, scale):
    scores = (
        jnp.einsum("qhd,khd->hqk", query_heads, key_heads, preferred_element_type=jnp.float32)
        * scale
    )
    return jnp.where(allowed, scores, -1e30)


def matmul(left, right):
    return jnp.dot(left, right, preferred_element_type=jnp.float32)


def column_sums(values):
    return jnp.sum(values.astype(jnp.float32), axis=0)


def on_device(
    tokens,
    segments,
    cotangent,
    query_weight,
    query_bias,
    key_weight,
    value_weight,
    value_bias,
    output_weight,
    output_bias,
    first_gain,
    first_shift,
    inner_weight,
    inner_bias,
    outer_weight,
    outer_bias,
    second_gain,
    second_shift,
):
    shards = (
        query_weight,
        query_bias,
        key_weight,
        value_weight,
        value_bias,
        output_weight,
        output_bias,
        first_gain,
        first_shift,
        inner_weight,
        inner_bias,
        outer_weight,
        outer_bias,
        second_gain,
        second_shift,
    )
    micro = tokens.shape[0]
    local = tokens.shape[1]
    width = tokens.shape[2]
    scale = 1.0 / math.sqrt(HEAD)
    offset = lax.axis_index("ctx") * local
    outputs = []
    input_grads = []
    totals = None
    for micro_step in range(micro):
        params = fetch_weights(shards)
        source = tokens[micro_step]
        seg_whole = segments[micro_step]
        seg_local = lax.dynamic_slice_in_dim(seg_whole, offset, local)
        allowed = seg_local[None, :, None] == seg_whole[None, None, :]
        queries = (matmul(source, params[0]) + params[1].astype(jnp.float32)).astype(jnp.bfloat16)
        keys_local = matmul(source, params[2]).astype(jnp.bfloat16)
        values_local = (matmul(source, params[3]) + params[4].astype(jnp.float32)).astype(
            jnp.bfloat16
        )
        keys_whole, values_whole = (
            lax.all_gather(keys_local, "ctx", axis=0, tiled=True),
            lax.all_gather(values_local, "ctx", axis=0, tiled=True),
        )
        query_heads = queries.reshape(local, HEADS, HEAD)
        key_heads = keys_whole.reshape(-1, HEADS, HEAD)
        value_heads = values_whole.reshape(-1, HEADS, HEAD)
        masked = masked_scores(query_heads, key_heads, allowed, scale)
        largest = jnp.max(masked, axis=-1, keepdims=True)
        logsum = largest + jnp.log(jnp.sum(jnp.exp(masked - largest), axis=-1, keepdims=True))
        probs_low = jnp.exp(masked - logsum).astype(jnp.bfloat16)
        mixed = (
            jnp.einsum("hqk,khd->qhd", probs_low, value_heads, preferred_element_type=jnp.float32)
            .reshape(local, width)
            .astype(jnp.bfloat16)
        )
        pre = source.astype(jnp.float32) + matmul(mixed, params[5]) + params[6].astype(jnp.float32)
        first, first_back = jax.vjp(
            layer_norm, pre, params[7].astype(jnp.float32), params[8].astype(jnp.float32)
        )
        first_low = first.astype(jnp.bfloat16)
        inner = matmul(first_low, params[9]) + params[10].astype(jnp.float32)
        active, gelu_back = jax.vjp(gelu_exact, inner)
        active_low = active.astype(jnp.bfloat16)
        total = first + matmul(active_low, params[11]) + params[12].astype(jnp.float32)
        result, second_back = jax.vjp(
            layer_norm, total, params[13].astype(jnp.float32), params[14].astype(jnp.float32)
        )
        outputs.append(result.astype(jnp.bfloat16))
        later = (
            lax.all_gather(shards[0], ("dp", "ctx"), axis=0, tiled=True),
            lax.all_gather(shards[1], ("dp", "ctx"), axis=0, tiled=True),
            lax.all_gather(shards[2], ("dp", "ctx"), axis=0, tiled=True),
            lax.all_gather(shards[3], ("dp", "ctx"), axis=0, tiled=True),
            lax.all_gather(shards[4], ("dp", "ctx"), axis=0, tiled=True),
            lax.all_gather(shards[5], ("dp", "ctx"), axis=0, tiled=True),
            lax.all_gather(shards[6], ("dp", "ctx"), axis=0, tiled=True),
            lax.all_gather(shards[7], ("dp", "ctx"), axis=0, tiled=True),
            lax.all_gather(shards[8], ("dp", "ctx"), axis=0, tiled=True),
            lax.all_gather(shards[9], ("dp", "ctx"), axis=0, tiled=True),
            lax.all_gather(shards[10], ("dp", "ctx"), axis=0, tiled=True),
            lax.all_gather(shards[11], ("dp", "ctx"), axis=0, tiled=True),
            lax.all_gather(shards[12], ("dp", "ctx"), axis=0, tiled=True),
            lax.all_gather(shards[13], ("dp", "ctx"), axis=0, tiled=True),
            lax.all_gather(shards[14], ("dp", "ctx"), axis=0, tiled=True),
        )
        d_total, d_second_gain, d_second_shift = second_back(
            cotangent[micro_step].astype(jnp.float32)
        )
        d_outer = d_total.astype(jnp.bfloat16)
        g_outer_weight = jnp.einsum(
            "tf,td->fd", active_low, d_outer, preferred_element_type=jnp.float32
        )
        g_outer_bias = column_sums(d_outer)
        d_active = jnp.einsum("td,fd->tf", d_outer, later[11], preferred_element_type=jnp.float32)
        d_inner = gelu_back(d_active)[0].astype(jnp.bfloat16)
        g_inner_weight = jnp.einsum(
            "td,tf->df", first_low, d_inner, preferred_element_type=jnp.float32
        )
        g_inner_bias = column_sums(d_inner)
        d_first = (
            jnp.einsum("tf,df->td", d_inner, later[9], preferred_element_type=jnp.float32) + d_total
        )
        d_pre, d_first_gain, d_first_shift = first_back(d_first)
        d_attended = d_pre.astype(jnp.bfloat16)
        g_output_weight = jnp.einsum(
            "td,te->de", mixed, d_attended, preferred_element_type=jnp.float32
        )
        g_output_bias = column_sums(d_attended)
        d_mixed = (
            jnp.einsum("te,de->td", d_attended, later[5], preferred_element_type=jnp.float32)
            .astype(jnp.bfloat16)
            .reshape(local, HEADS, HEAD)
        )
        again = masked_scores(query_heads, key_heads, allowed, scale)
        probs = jnp.exp(again - logsum)
        d_probs = jnp.einsum(
            "qhd,khd->hqk", d_mixed, value_heads, preferred_element_type=jnp.float32
        )
        row_sums = jnp.sum(probs * d_probs, axis=-1, keepdims=True)
        d_scores = (probs * (d_probs - row_sums)).astype(jnp.bfloat16)
        d_queries = (
            (
                jnp.einsum("hqk,khd->qhd", d_scores, key_heads, preferred_element_type=jnp.float32)
                * scale
            )
            .reshape(local, width)
            .astype(jnp.bfloat16)
        )
        probs_low = probs.astype(jnp.bfloat16)
        key_terms = (
            jnp.einsum("hqk,qhd->khd", d_scores, query_heads, preferred_element_type=jnp.float32)
            * scale
        ).reshape(-1, width)
        value_terms = jnp.einsum(
            "hqk,qhd->khd", probs_low, d_mixed, preferred_element_type=jnp.float32
        ).reshape(-1, width)
        d_keys, d_values = (
            lax.psum_scatter(
                key_terms.astype(jnp.bfloat16), "ctx", scatter_dimension=0, tiled=True
            ).astype(jnp.float32),
            lax.psum_scatter(
                value_terms.astype(jnp.bfloat16), "ctx", scatter_dimension=0, tiled=True
            ).astype(jnp.float32),
        )
        d_keys = d_keys.astype(jnp.bfloat16)
        d_values = d_values.astype(jnp.bfloat16)
        g_query_weight = jnp.einsum(
            "td,te->de", source, d_queries, preferred_element_type=jnp.float32
        )
        g_query_bias = column_sums(d_queries)
        g_key_weight = jnp.einsum("td,te->de", source, d_keys, preferred_element_type=jnp.float32)
        g_value_weight = jnp.einsum(
            "td,te->de", source, d_values, preferred_element_type=jnp.float32
        )
        g_value_bias = column_sums(d_values)
        d_input = d_pre + jnp.einsum(
            "te,de->td", d_queries, later[0], preferred_element_type=jnp.float32
        )
        d_input = d_input + jnp.einsum(
            "te,de->td", d_keys, later[2], preferred_element_type=jnp.float32
        )
        d_input = d_input + jnp.einsum(
            "te,de->td", d_values, later[3], preferred_element_type=jnp.float32
        )
        input_grads.append(d_input)
        local_grads = (
            g_query_weight,
            g_query_bias,
            g_key_weight,
            g_value_weight,
            g_value_bias,
            g_output_weight,
            g_output_bias,
            d_first_gain,
            d_first_shift,
            g_inner_weight,
            g_inner_bias,
            g_outer_weight,
            g_outer_bias,
            d_second_gain,
            d_second_shift,
        )
        totals = local_grads if totals is None else jax.tree.map(jnp.add, totals, local_grads)
    owned = lax.psum_scatter(totals, ("dp", "ctx"), scatter_dimension=0, tiled=True)
    return (
        jnp.stack(outputs),
        jnp.stack(input_grads),
        owned[0],
        owned[1],
        owned[2],
        owned[3],
        owned[4],
        owned[5],
        owned[6],
        owned[7],
        owned[8],
        owned[9],
        owned[10],
        owned[11],
        owned[12],
        owned[13],
        owned[14],
    )


def solution(mesh):
    return jax.shard_map(
        on_device,
        mesh=mesh,
        in_specs=(
            P("dp", "ctx", None),
            P("dp", None),
            P("dp", "ctx", None),
            P(("dp", "ctx"), None),
            P(("dp", "ctx")),
            P(("dp", "ctx"), None),
            P(("dp", "ctx"), None),
            P(("dp", "ctx")),
            P(("dp", "ctx"), None),
            P(("dp", "ctx")),
            P(("dp", "ctx")),
            P(("dp", "ctx")),
            P(("dp", "ctx"), None),
            P(("dp", "ctx")),
            P(("dp", "ctx"), None),
            P(("dp", "ctx")),
            P(("dp", "ctx")),
            P(("dp", "ctx")),
        ),
        out_specs=(
            P("dp", "ctx", None),
            P("dp", "ctx", None),
            P(("dp", "ctx"), None),
            P(("dp", "ctx")),
            P(("dp", "ctx"), None),
            P(("dp", "ctx"), None),
            P(("dp", "ctx")),
            P(("dp", "ctx"), None),
            P(("dp", "ctx")),
            P(("dp", "ctx")),
            P(("dp", "ctx")),
            P(("dp", "ctx"), None),
            P(("dp", "ctx")),
            P(("dp", "ctx"), None),
            P(("dp", "ctx")),
            P(("dp", "ctx")),
            P(("dp", "ctx")),
        ),
        check_vma=False,
    )
```

profile of v0, /device:TPU:0, one launch (start us, length us, event | category | flops | bytes accessed | tf_op | source)
XLA Modules:
  0.0 1531.9 jit_solution(13532980301998678464)
XLA Ops:
  9.6 58.2 %all-gather.17.cloned.1.call-done = bf16[768,768]{1,0:T(8,128)(2,1)} async-done(((bf16[24,768]{1,0:T(8,128)(2,1)}), bf16[768,768]{1,0:T(8,128)(2,1)}) %all-gather.17.cloned.1.call-update) | async-done | bytes 1179664 | tf_op jit(solution)/shard_map/all_gather | solution.py:27
  73.2 39.7 %all-reduce.19 = (bf16[768]{0:T(1024)(128)(2,1)S(1)}, bf16[768]{0:T(1024)(128)(2,1)S(1)}, bf16[768]{0:T(1024)(128)(2,1)S(1)}, bf16[768]{0:T(1024)(128)(2,1)S(1)}...) all-reduce(bf16[768]{0:T(1024)(128)(2,1)S(1)} %dynamic-update-slice, ...), channel_id=1, replica_groups=mesh['dp'=8,'ctx'=4] {'dp','ctx'}, use_global_device_ids=true, to_apply=%add | all-reduce | flops 9216 | bytes 36864
  136.6 42.9 %all-gather.15.cloned.1.call-done = bf16[768,768]{1,0:T(8,128)(2,1)} async-done(((bf16[24,768]{1,0:T(8,128)(2,1)}), bf16[768,768]{1,0:T(8,128)(2,1)}) %all-gather.15.cloned.1.call-update) | async-done | bytes 1179664 | tf_op jit(solution)/shard_map/all_gather | solution.py:25
  213.2 22.5 %fusion.1 = (f32[12,512]{1,0:T(8,128)S(1)}, f32[12,512,2048]{2,1,0:T(8,128)}) fusion(pred[512,2048]{1,0:T(8,128)(4,1)S(1)} %broadcast_compare_fusion, bf16[512,12,64]{0,2,1:T(8,128)(2,1)S(1)} %bitcast.203, bf16[2048,12,64]{0,2,1:T(8,128)(2,1)} %bitcast.193), kind=kOutput, calls=%fused_computation.11 | convolution fusion | flops 1648355328 | bytes 55336960 | tf_op jit(solution)/shard_map/qhd,khd->hqk/dot_general | solution.py:45
  235.7 21.9 %exponential_reduce_fusion = f32[12,512]{1,0:T(8,128)S(1)} fusion(f32[12,512,2048]{2,1,0:T(8,128)} %get-tuple-element.145, f32[12,512]{1,0:T(8,128)S(1)} %get-tuple-element.144, pred[512,2048]{1,0:T(8,128)(4,1)S(1)} %broadcast_compare_fusion), kind=kLoop, calls=%fused_computation.5 | loop fusion | flops 50325504 | bytes 51429376 | tf_op jit(solution)/shard_map/reduce_sum | solution.py:124
  262.3 20.3 %convolution_convert_fusion.2 = bf16[12,64,512]{2,1,0:T(8,128)(2,1)S(1)} fusion(bf16[2048,12,64]{0,2,1:T(8,128)(2,1)} %bitcast.197, f32[12,512,2048]{2,1,0:T(8,128)} %get-tuple-element.145, f32[12,512]{1,0:T(8,128)S(1)} %log_add_fusion, pred[512,2048]{1,0:T(8,128)(4,1)S(1)} %broadcast_compare_fusion), kind=kOutput, calls=%fused_computation.122 | convolution fusion | flops 1661337600 | bytes 55336960 | tf_op jit(solution)/shard_map/hqk,khd->qhd/dot_general | solution.py:127
  299.1 25.5 %all-gather.19.cloned.1.call-done = bf16[2048,768]{1,0:T(8,128)(2,1)} async-done(((bf16[512,768]{1,0:T(8,128)(2,1)}), bf16[2048,768]{1,0:T(8,128)(2,1)}) %all-gather.19.cloned.1.call-update) | async-done | bytes 3145744 | tf_op jit(solution)/shard_map/all_gather | solution.py:116
  329.4 22.7 %fusion = (f32[12,512]{1,0:T(8,128)S(1)}, f32[12,512,2048]{2,1,0:T(8,128)}) fusion(pred[512,2048]{1,0:T(8,128)(4,1)S(1)} %broadcast_compare_fusion.1, bf16[512,12,64]{0,2,1:T(8,128)(2,1)S(1)} %bitcast.205, bf16[2048,12,64]{0,2,1:T(8,128)(2,1)} %bitcast.195), kind=kOutput, calls=%fused_computation.10 | convolution fusion | flops 1648355328 | bytes 55336960 | tf_op jit(solution)/shard_map/qhd,khd->hqk/dot_general | solution.py:45
  352.1 22.0 %exponential_reduce_fusion.1 = f32[12,512]{1,0:T(8,128)S(1)} fusion(f32[12,512,2048]{2,1,0:T(8,128)} %get-tuple-element.141, f32[12,512]{1,0:T(8,128)S(1)} %get-tuple-element.140, pred[512,2048]{1,0:T(8,128)(4,1)S(1)} %broadcast_compare_fusion.1), kind=kLoop, calls=%fused_computation.8 | loop fusion | flops 50325504 | bytes 51429376 | tf_op jit(solution)/shard_map/reduce_sum | solution.py:124
  378.9 20.7 %convolution_convert_fusion.3 = bf16[12,64,512]{2,1,0:T(8,128)(2,1)S(1)} fusion(bf16[2048,12,64]{0,2,1:T(8,128)(2,1)} %bitcast.199, f32[12,512,2048]{2,1,0:T(8,128)} %get-tuple-element.141, f32[12,512]{1,0:T(8,128)S(1)} %log_add_fusion.1, pred[512,2048]{1,0:T(8,128)(4,1)S(1)} %broadcast_compare_fusion.1), kind=kOutput, calls=%fused_computation.123 | convolution fusion | flops 1661337600 | bytes 55336960 | tf_op jit(solution)/shard_map/hqk,khd->qhd/dot_general | solution.py:127
  429.2 35.1 %multiply_convert_fusion.5 = (bf16[512,3072]{1,0:T(8,128)(2,1)}, f32[512,3072]{1,0:T(8,128)}, bf16[512,3072]{1,0:T(8,128)(2,1)}, f32[512,3072]{1,0:T(8,128)}, f32[512,3072]{1,0:T(8,128)}) fusion(f32[3072]{0:T(1024)S(1)} %convert_element_type.260, f32[512,3072]{1,0:T(8,128)S(1)} %fusion.76, bf16[768,3072]{1,0:T(8,128)(2,1)S(1)} %copy-done.85, ...), kind=kOutput, calls=%fused_computation.37 | convolution fusion | flops 2625503232 | bytes 37771264 | tf_op jit(solution)/shard_map/dot_general | solution.py:52
  464.3 21.6 %all-gather.25.cloned.1.call-done = bf16[3072,768]{1,0:T(8,128)(2,1)} async-done(((bf16[96,768]{1,0:T(8,128)(2,1)}), bf16[3072,768]{1,0:T(8,128)(2,1)}) %all-gather.25.cloned.1.call-update) | async-done | bytes 4718608 | tf_op jit(solution)/shard_map/all_gather | solution.py:36
  544.8 22.6 %convolution_convert_fusion.1 = bf16[12,64,2048]{2,1,0:T(8,128)(2,1)} fusion(bf16[512,12,64]{0,2,1:T(8,128)(2,1)S(1)} %bitcast.213, f32[12,512,2048]{2,1,0:T(8,128)} %get-tuple-element.141, f32[12,512]{1,0:T(8,128)S(1)} %log_add_fusion.1, pred[512,2048]{1,0:T(8,128)(4,1)S(1)} %broadcast_compare_fusion.1), kind=kOutput, calls=%fused_computation.55 | convolution fusion | flops 1662517248 | bytes 55336960 | tf_op jit(solution)/shard_map/hqk,qhd->khd/dot_general | solution.py:209
  575.5 22.9 %convolution_convert_fusion = bf16[12,64,2048]{2,1,0:T(8,128)(2,1)} fusion(bf16[512,12,64]{0,2,1:T(8,128)(2,1)S(1)} %bitcast.211, f32[12,512,2048]{2,1,0:T(8,128)} %get-tuple-element.145, f32[12,512]{1,0:T(8,128)S(1)} %copy-done.52, pred[512,2048]{1,0:T(8,128)(4,1)S(1)} %copy-done.1), kind=kOutput, calls=%fused_computation.54 | convolution fusion | flops 1662517248 | bytes 55336960 | tf_op jit(solution)/shard_map/hqk,qhd->khd/dot_general | solution.py:209
  599.5 38.1 %multiply_reduce_fusion.1 = (f32[12,512]{1,0:T(8,128)S(1)}, f32[12,512,2048]{2,1,0:T(8,128)}) fusion(f32[12,512,2048]{2,1,0:T(8,128)} %get-tuple-element.141, f32[12,512]{1,0:T(8,128)S(1)} %log_add_fusion.1, pred[512,2048]{1,0:T(8,128)(4,1)S(1)} %broadcast_compare_fusion.1, bf16[512,12,64]{0,2,1:T(8,128)(2,1)S(1)} %bitcast.214, ...), kind=kOutput, calls=%fused_computation.3 | convolution fusion | flops 1673521152 | bytes 105693184 | tf_op jit(solution)/shard_map/qhd,khd->hqk/dot_general | solution.py:191
  637.6 40.5 %multiply_convert_fusion.1 = bf16[12,512,2048]{2,1,0:T(8,128)(2,1)} fusion(f32[12,512,2048]{2,1,0:T(8,128)} %get-tuple-element.157, f32[12,512,2048]{2,1,0:T(8,128)} %get-tuple-element.141, f32[12,512]{1,0:T(8,128)S(1)} %get-tuple-element.156, f32[12,512]{1,0:T(8,128)S(1)} %log_add_fusion.1, pred[512,2048]{1,0:T(8,128)(4,1)S(1)} %broadcast_compare_fusion.1), kind=kLoop, calls=%fused_computation.2 | loop fusion | flops 75497472 | bytes 126926848 | tf_op jit(solution)/shard_map/convert_element_type | solution.py:195
  693.6 38.4 %multiply_reduce_fusion = (f32[12,512]{1,0:T(8,128)S(1)}, f32[12,512,2048]{2,1,0:T(8,128)}) fusion(f32[12,512,2048]{2,1,0:T(8,128)} %get-tuple-element.145, f32[12,512]{1,0:T(8,128)S(1)} %copy-done.52, pred[512,2048]{1,0:T(8,128)(4,1)S(1)} %copy-done.1, bf16[512,12,64]{0,2,1:T(8,128)(2,1)S(1)} %bitcast.212, bf16[2048,12,64]{0,2,1:T(8,128)(2,1)} %bitcast.198), kind=kOutput, calls=%fused_computation.1 | convolution fusion | flops 1673521152 | bytes 105693184 | tf_op jit(solution)/shard_map/qhd,khd->hqk/dot_general | solution.py:191
  731.9 40.4 %multiply_convert_fusion = bf16[12,512,2048]{2,1,0:T(8,128)(2,1)} fusion(f32[12,512,2048]{2,1,0:T(8,128)} %get-tuple-element.155, f32[12,512,2048]{2,1,0:T(8,128)} %get-tuple-element.145, f32[12,512]{1,0:T(8,128)S(1)} %get-tuple-element.154, f32[12,512]{1,0:T(8,128)S(1)} %copy-done.52, pred[512,2048]{1,0:T(8,128)(4,1)S(1)} %copy-done.1), kind=kLoop, calls=%fused_computation | loop fusion | flops 75497472 | bytes 126926848 | tf_op jit(solution)/shard_map/convert_element_type | solution.py:195
  883.0 40.9 %all-reduce.18 = (f32[768]{0:T(1024)S(1)}, f32[768]{0:T(1024)S(1)}, f32[768]{0:T(1024)S(1)}, f32[768]{0:T(1024)S(1)}, f32[768]{0:T(1024)S(1)}, /*index=5*/f32[30...) all-reduce(f32[768]{0:T(1024)S(1)} %add.332, ...), channel_id=7, replica_groups=mesh['dp'=8,'ctx'=4] {'dp','ctx'}, use_global_device_ids=true, to_apply=%region_29.30.clone | all-reduce | flops 9216 | bytes 73728
  937.0 96.0 %reduce-scatter.31.cloned.1.call-done = f32[24,768]{1,0:T(8,128)} async-done(((f32[768,768]{1,0:T(8,128)}), f32[24,768]{1,0:T(8,128)}) %reduce-scatter.31.cloned.1.call-update) | async-done | bytes 73744
  1033.0 104.4 %reduce-scatter.35.cloned.1.call-done = f32[24,768]{1,0:T(8,128)} async-done(((f32[768,768]{1,0:T(8,128)}), f32[24,768]{1,0:T(8,128)}) %reduce-scatter.35.cloned.1.call-update) | async-done | bytes 73744
  1137.3 104.3 %reduce-scatter.33.cloned.1.call-done = f32[24,768]{1,0:T(8,128)} async-done(((f32[768,768]{1,0:T(8,128)}), f32[24,768]{1,0:T(8,128)}) %reduce-scatter.33.cloned.1.call-update) | async-done | bytes 73744
  1241.6 141.8 %reduce-scatter.27.cloned.1.call-done = f32[24,3072]{1,0:T(8,128)} async-done(((f32[768,3072]{1,0:T(8,128)}), f32[24,3072]{1,0:T(8,128)}) %reduce-scatter.27.cloned.1.call-update) | async-done | bytes 294928 | tf_op jit(solution)/shard_map/reduce_scatter | solution.py:259
  1383.4 141.4 %reduce-scatter.29.cloned.1.call-done = f32[96,768]{1,0:T(8,128)} async-done(((f32[3072,768]{1,0:T(8,128)}), f32[96,768]{1,0:T(8,128)}) %reduce-scatter.29.cloned.1.call-update) | async-done | bytes 294928 | tf_op jit(solution)/shard_map/reduce_scatter | solution.py:259
  (389 shorter events, 331.3 us)
Async XLA Ops:
  7.3 60.4 %all-gather.17.cloned.1.call-start = ((), (), s32[]{:S(2)}) async-start(), calls=%async_computation.13 | async-start | bytes 1216512 | tf_op jit(solution)/shard_map/all_gather | solution.py:27
  8.0 115.6 %all-gather.11.cloned.1.call-start = ((), (), s32[]{:S(2)}) async-start(), calls=%async_computation.10 | async-start | bytes 1216512 | tf_op jit(solution)/shard_map/all_gather | solution.py:28
  8.8 170.7 %all-gather.15.cloned.1.call-start = ((), (), s32[]{:S(2)}) async-start(), calls=%async_computation.12 | async-start | bytes 1216512 | tf_op jit(solution)/shard_map/all_gather | solution.py:25
  9.5 198.9 %all-gather.29.cloned.1.call-start = ((), (), s32[]{:S(2)}) async-start(), calls=%async_computation.19 | async-start | bytes 3932160 | tf_op jit(solution)/shard_map/all_gather | solution.py:116
  71.0 186.7 %all-gather.27.cloned.1.call-start = ((), (), s32[]{:S(2)}) async-start(), calls=%async_computation.18 | async-start | bytes 3932160 | tf_op jit(solution)/shard_map/all_gather | solution.py:117
  126.6 169.1 %all-gather.21.cloned.1.call-start = ((), (), s32[]{:S(2)}) async-start(), calls=%async_computation.15 | async-start | bytes 1216512 | tf_op jit(solution)/shard_map/all_gather | solution.py:30
  127.2 197.5 %all-gather.19.cloned.1.call-start = ((), (), s32[]{:S(2)}) async-start(), calls=%async_computation.14 | async-start | bytes 3932160 | tf_op jit(solution)/shard_map/all_gather | solution.py:116
  130.2 243.9 %all-gather.13.cloned.1.call-start = ((), (), s32[]{:S(2)}) async-start(), calls=%async_computation.11 | async-start | bytes 3932160 | tf_op jit(solution)/shard_map/all_gather | solution.py:117
  132.0 289.3 %all-gather.23.cloned.1.call-start = ((), (), s32[]{:S(2)}) async-start(), calls=%async_computation.16 | async-start | bytes 4866048 | tf_op jit(solution)/shard_map/all_gather | solution.py:34
  132.7 353.2 %all-gather.25.cloned.1.call-start = ((), (), s32[]{:S(2)}) async-start(), calls=%async_computation.17 | async-start | bytes 4866048 | tf_op jit(solution)/shard_map/all_gather | solution.py:36
  133.3 698.6 %reduce-scatter.19.cloned.1.call-start = ((), (), s32[]{:S(2)}) async-start(), calls=%async_computation.21 | async-start | bytes 3932160 | tf_op jit(solution)/shard_map/reduce_scatter | solution.py:216
  133.4 405.3 %copy-start.53 = (f32[768]{0:T(1024)}, f32[768]{0:T(1024)S(1)}, u32[]{:S(2)}) copy-start(f32[768]{0:T(1024)S(1)} %convert_element_type.257) | copy-start | bytes 9220
  133.4 359.5 %copy-start.55 = (f32[768]{0:T(1024)}, f32[768]{0:T(1024)S(1)}, u32[]{:S(2)}) copy-start(f32[768]{0:T(1024)S(1)} %convert_element_type.258) | copy-start | bytes 9220
  299.1 239.6 %copy-start.57 = (f32[512]{0:T(512)}, f32[512]{0:T(512)S(1)}, u32[]{:S(2)}) copy-start(f32[512]{0:T(512)S(1)} %broadcast_multiply_fusion.1) | copy-start | bytes 6148
  400.5 138.2 %copy-start.62 = (f32[512]{0:T(512)}, f32[512]{0:T(512)S(1)}, u32[]{:S(2)}) copy-start(f32[512]{0:T(512)S(1)} %broadcast_multiply_fusion.3) | copy-start | bytes 6148
  567.5 267.8 %reduce-scatter.23.cloned.1.call-start = ((), (), s32[]{:S(2)}) async-start(), calls=%async_computation.23 | async-start | bytes 3932160 | tf_op jit(solution)/shard_map/reduce_scatter | solution.py:216
  598.4 244.2 %reduce-scatter.17.cloned.1.call-start = ((), (), s32[]{:S(2)}) async-start(), calls=%async_computation.20 | async-start | bytes 3932160 | tf_op jit(solution)/shard_map/reduce_scatter | solution.py:213
  692.5 153.5 %reduce-scatter.21.cloned.1.call-start = ((), (), s32[]{:S(2)}) async-start(), calls=%async_computation.22 | async-start | bytes 3932160 | tf_op jit(solution)/shard_map/reduce_scatter | solution.py:213
  786.7 150.3 %reduce-scatter.25.cloned.1.call-start = ((), (), s32[]{:S(2)}) async-start(), calls=%async_computation.24 | async-start | bytes 2433024 | tf_op jit(solution)/shard_map/reduce_scatter | solution.py:259
  792.6 240.4 %reduce-scatter.31.cloned.1.call-start = ((), (), s32[]{:S(2)}) async-start(), calls=%async_computation.27 | async-start | bytes 2433024
  831.9 305.5 %reduce-scatter.35.cloned.1.call-start = ((), (), s32[]{:S(2)}) async-start(), calls=%async_computation.29 | async-start | bytes 2433024
  842.6 399.0 %reduce-scatter.33.cloned.1.call-start = ((), (), s32[]{:S(2)}) async-start(), calls=%async_computation.28 | async-start | bytes 2433024
  853.4 530.1 %reduce-scatter.27.cloned.1.call-start = ((), (), s32[]{:S(2)}) async-start(), calls=%async_computation.25 | async-start | bytes 9732096 | tf_op jit(solution)/shard_map/reduce_scatter | solution.py:259
  864.8 660.1 %reduce-scatter.29.cloned.1.call-start = ((), (), s32[]{:S(2)}) async-start(), calls=%async_computation.26 | async-start | bytes 9732096 | tf_op jit(solution)/shard_map/reduce_scatter | solution.py:259
  (98 other events, 1690.4 us)
Sparse Core Ops, SparseCore 0:
  11.0 56.6 all-gather.16
  70.6 52.9 all-gather.10
  126.5 52.9 all-gather.14
  180.9 27.4 all-gather.28
  210.4 28.4 all-gather.26
  241.7 53.9 all-gather.20
  297.2 27.4 all-gather.18
  326.2 28.4 all-gather.12
  357.7 63.5 all-gather.22
  424.0 61.8 all-gather.24
  567.6 36.0 reduce-scatter.18
  606.1 37.7 reduce-scatter.22
  692.6 36.9 reduce-scatter.16
  786.8 36.1 reduce-scatter.20
  828.8 99.8 reduce-scatter.24
  934.4 98.5 reduce-scatter.30
  1038.7 98.6 reduce-scatter.34
  1143.0 98.5 reduce-scatter.32
  1248.1 135.2 reduce-scatter.26
  1389.8 135.0 reduce-scatter.28
where the time goes:
time: 1540 us; the launch traced here: 1530 us
  waiting for transfers between devices  801 us (52%)
  matrix products  433 us (28%)
  other arithmetic  145 us (9%)
  blocking collectives  80.6 us (5%)
  local copies, waits for them, and re-layouts  54.7 us (4%)
  between operations  15.9 us (1%)
    unnamed x23, waiting for transfers between devices  309 us
    reduce_scatter x3, waiting for transfers between devices, on_device(): lax.psum_scatter(totals, ('dp', 'ctx'), scatter_dimension=0, tiled=True)  283 us
    convert_element_type x2, other arithmetic, on_device(): d_scores = (probs * (d_probs - row_sums)).astype(jnp.bfloat16)  80.9 us
    unnamed x2, blocking collectives  80.6 us
    dot_general x2, matrix products, on_device(): jnp.einsum('qhd,khd->hqk', d_mixed, value_heads, preferred_element_type=j...  76.5 us
    dot_general x12, matrix products, matmul(): return jnp.dot(left, right, preferred_element_type=jnp.float32)  71.8 us
    all_gather x1, waiting for transfers between devices, fetch_weights(): lax.all_gather(shards[2], ('dp', 'ctx'), axis=0, tiled=True)  58.2 us
    dot_general x2, matrix products, on_device(): jnp.einsum('hqk,qhd->khd', probs_low, d_mixed, preferred_element_type=jnp...  45.5 us
  transfers between devices with their start and end apart: 20, of which 13 were waited for; matrix products, arithmetic and copies ran while one was open for 35% of the time, Pallas kernels for 0%

commit v1 on v0

--- a/solution.py
+++ b/solution.py
@@ -7,6 +7,19 @@
 HEADS = 12
 HEAD = 64
 epsilon = 1e-05
+
+
+def gather_around(value, axis, dim):
+    ways = lax.axis_size(axis)
+    up = [(d, (d + 1) % ways) for d in range(ways)]
+    down = [(d, (d - 1) % ways) for d in range(ways)]
+    earlier, later = ([value], [value])
+    for _ in range(ways // 2):
+        earlier.append(lax.ppermute(earlier[-1], axis, up))
+    for _ in range((ways - 1) // 2):
+        later.append(lax.ppermute(later[-1], axis, down))
+    line = jnp.concatenate([*earlier[::-1], *later[1:]], axis=dim)
+    return jnp.roll(line, (lax.axis_index(axis) - ways // 2) * value.shape[dim], axis=dim)
 
 
 def layer_norm(values, gain, shift):
@@ -113,7 +126,7 @@
             jnp.bfloat16
         )
         keys_whole, values_whole = (
-            lax.all_gather(keys_local, "ctx", axis=0, tiled=True),
+            gather_around(keys_local, "ctx", 0),
             lax.all_gather(values_local, "ctx", axis=0, tiled=True),
         )
         query_heads = queries.reshape(local, HEADS, HEAD)

time: 1540 us -> 1490 us (0.968)
  waiting for transfers between devices: 801 us -> 717 us
  other arithmetic: 145 us -> 168 us
    all_gather x2 -> x0, waiting for transfers between devices: 43.7 us -> none  [on_device(): lax.all_gather(keys_local, 'ctx', axis=0, tiled=True)]
    ppermute x0 -> x6, waiting for transfers between devices: none -> 22.6 us  [the longest x4 22.6 us: gather_around(): earlier.append(lax.ppermute(earlier[-1], axis, up))]
    concatenate x0 -> x2, other arithmetic: none -> 21.8 us  [gather_around(): jnp.roll(line, (lax.axis_index(axis) - ways // 2) * value.shape[dim], axi...]
    all_gather x1, waiting for transfers between devices: 19.2 us -> 0.02 us  [fetch_weights(): lax.all_gather(shards[9], ('dp', 'ctx'), axis=0, tiled=True)]
    unnamed x234 -> x218, local copies, waits for them, and re-layouts: 29.8 us -> 35.3 us
    unnamed x23 -> x21, waiting for transfers between devices: 309 us -> 310 us
  transfers between devices with their start and end apart: 20 -> 24, of which waited for: 13 -> 11; matrix products, arithmetic and copies ran while one was open for 35% -> 38% of each run, Pallas kernels for 0% -> 0%
where the time goes in v1:
time: 1490 us; the launch traced here: 1480 us
  waiting for transfers between devices  717 us (48%)
  matrix products  434 us (29%)
  other arithmetic  168 us (11%)
  blocking collectives  82.8 us (6%)
  local copies, waits for them, and re-layouts  59.8 us (4%)
  between operations  16.1 us (1%)
    unnamed x21, waiting for transfers between devices  310 us
    reduce_scatter x3, waiting for transfers between devices, on_device(): lax.psum_scatter(totals, ('dp', 'ctx'), scatter_dimension=0, tiled=True)  283 us
    unnamed x2, blocking collectives  82.8 us
    convert_element_type x2, other arithmetic, on_device(): d_scores = (probs * (d_probs - row_sums)).astype(jnp.bfloat16)  81 us
    dot_general x2, matrix products, on_device(): jnp.einsum('qhd,khd->hqk', d_mixed, value_heads, preferred_element_type=j...  76.6 us
    dot_general x12, matrix products, matmul(): return jnp.dot(left, right, preferred_element_type=jnp.float32)  71.9 us
    all_gather x1, waiting for transfers between devices, fetch_weights(): lax.all_gather(shards[2], ('dp', 'ctx'), axis=0, tiled=True)  48.4 us
    dot_general x2, matrix products, on_device(): jnp.einsum('hqk,qhd->khd', probs_low, d_mixed, preferred_element_type=jnp...  45.6 us
  transfers between devices with their start and end apart: 24, of which 11 were waited for; matrix products, arithmetic and copies ran while one was open for 38% of the time, Pallas kernels for 0%

profile of v1, /device:TPU:0, one launch (start us, length us, event | category | flops | bytes accessed | tf_op | source)
XLA Modules:
  0.0 1482.0 jit_solution(12422888459164691713)
XLA Ops:
  17.0 42.5 %all-reduce.19 = (bf16[768]{0:T(1024)(128)(2,1)S(1)}, bf16[768]{0:T(1024)(128)(2,1)S(1)}, bf16[768]{0:T(1024)(128)(2,1)S(1)}, bf16[768]{0:T(1024)(128)(2,1)S(1)}...) all-reduce(bf16[768]{0:T(1024)(128)(2,1)S(1)} %dynamic-update-slice, ...), channel_id=1, replica_groups=mesh['dp'=8,'ctx'=4] {'dp','ctx'}, use_global_device_ids=true, to_apply=%add | all-reduce | flops 9216 | bytes 36864
  75.3 48.4 %all-gather.15.cloned.1.call-done = bf16[768,768]{1,0:T(8,128)(2,1)} async-done(((bf16[24,768]{1,0:T(8,128)(2,1)}), bf16[768,768]{1,0:T(8,128)(2,1)}) %all-gather.15.cloned.1.call-update) | async-done | bytes 1179664 | tf_op jit(solution)/shard_map/all_gather | solution.py:40
  149.1 31.9 %all-gather.13.cloned.1.call-done = bf16[768,768]{1,0:T(8,128)(2,1)} async-done(((bf16[24,768]{1,0:T(8,128)(2,1)}), bf16[768,768]{1,0:T(8,128)(2,1)}) %all-gather.13.cloned.1.call-update) | async-done | bytes 1179664 | tf_op jit(solution)/shard_map/all_gather | solution.py:38
  233.0 22.7 %fusion.1 = (f32[12,512]{1,0:T(8,128)S(1)}, f32[12,512,2048]{2,1,0:T(8,128)}) fusion(pred[512,2048]{1,0:T(8,128)(4,1)S(1)} %broadcast_compare_fusion, bf16[512,12,64]{0,2,1:T(8,128)(2,1)S(1)} %bitcast.203, bf16[2048,12,64]{0,2,1:T(8,128)(2,1)} %bitcast.195), kind=kOutput, calls=%fused_computation.11 | convolution fusion | flops 1648355328 | bytes 55336960 | tf_op jit(solution)/shard_map/qhd,khd->hqk/dot_general | solution.py:58
  255.8 22.1 %exponential_reduce_fusion = f32[12,512]{1,0:T(8,128)S(1)} fusion(f32[12,512,2048]{2,1,0:T(8,128)} %get-tuple-element.146, f32[12,512]{1,0:T(8,128)S(1)} %get-tuple-element.145, pred[512,2048]{1,0:T(8,128)(4,1)S(1)} %broadcast_compare_fusion), kind=kLoop, calls=%fused_computation.5 | loop fusion | flops 50325504 | bytes 51429376 | tf_op jit(solution)/shard_map/reduce_sum | solution.py:137
  277.9 22.5 %fusion = (f32[12,512]{1,0:T(8,128)S(1)}, f32[12,512,2048]{2,1,0:T(8,128)}) fusion(pred[512,2048]{1,0:T(8,128)(4,1)S(1)} %broadcast_compare_fusion.1, bf16[512,12,64]{0,2,1:T(8,128)(2,1)S(1)} %bitcast.205, bf16[2048,12,64]{0,2,1:T(8,128)(2,1)} %bitcast.193), kind=kOutput, calls=%fused_computation.10 | convolution fusion | flops 1648355328 | bytes 55336960 | tf_op jit(solution)/shard_map/qhd,khd->hqk/dot_general | solution.py:58
  300.4 22.0 %exponential_reduce_fusion.1 = f32[12,512]{1,0:T(8,128)S(1)} fusion(f32[12,512,2048]{2,1,0:T(8,128)} %get-tuple-element.142, f32[12,512]{1,0:T(8,128)S(1)} %get-tuple-element.141, pred[512,2048]{1,0:T(8,128)(4,1)S(1)} %broadcast_compare_fusion.1), kind=kLoop, calls=%fused_computation.8 | loop fusion | flops 50325504 | bytes 51429376 | tf_op jit(solution)/shard_map/reduce_sum | solution.py:137
  327.1 20.6 %convolution_convert_fusion.2 = bf16[12,64,512]{2,1,0:T(8,128)(2,1)S(1)} fusion(bf16[2048,12,64]{0,2,1:T(8,128)(2,1)} %bitcast.197, f32[12,512,2048]{2,1,0:T(8,128)} %get-tuple-element.146, f32[12,512]{1,0:T(8,128)S(1)} %log_add_fusion, pred[512,2048]{1,0:T(8,128)(4,1)S(1)} %broadcast_compare_fusion), kind=kOutput, calls=%fused_computation.152 | convolution fusion | flops 1661337600 | bytes 55336960 | tf_op jit(solution)/shard_map/hqk,khd->qhd/dot_general | solution.py:140
  356.1 21.0 %convolution_convert_fusion.3 = bf16[12,64,512]{2,1,0:T(8,128)(2,1)S(1)} fusion(bf16[2048,12,64]{0,2,1:T(8,128)(2,1)} %bitcast.199, f32[12,512,2048]{2,1,0:T(8,128)} %get-tuple-element.142, f32[12,512]{1,0:T(8,128)S(1)} %log_add_fusion.1, pred[512,2048]{1,0:T(8,128)(4,1)S(1)} %broadcast_compare_fusion.1), kind=kOutput, calls=%fused_computation.153 | convolution fusion | flops 1661337600 | bytes 55336960 | tf_op jit(solution)/shard_map/hqk,khd->qhd/dot_general | solution.py:140
  387.8 34.9 %multiply_convert_fusion.5 = (bf16[512,3072]{1,0:T(8,128)(2,1)}, f32[512,3072]{1,0:T(8,128)}, bf16[512,3072]{1,0:T(8,128)(2,1)}, f32[512,3072]{1,0:T(8,128)}, f32[512,3072]{1,0:T(8,128)}) fusion(f32[3072]{0:T(1024)S(1)} %convert_element_type.260, f32[512,3072]{1,0:T(8,128)S(1)} %fusion.90, bf16[768,3072]{1,0:T(8,128)(2,1)S(1)} %copy-done.85, ...), kind=kOutput, calls=%fused_computation.53 | convolution fusion | flops 2625503232 | bytes 37771264 | tf_op jit(solution)/shard_map/dot_general | solution.py:65
  457.8 17.7 %convert_reduce_fusion.1 = (f32[3072]{0:T(1024)}, bf16[512,3072]{1,0:T(8,128)(2,1)}, f32[3072]{0:T(1024)}, bf16[512,3072]{1,0:T(8,128)(2,1)}) fusion(f32[512,3072]{1,0:T(8,128)} %get-tuple-element.122, f32[512,3072]{1,0:T(8,128)} %get-tuple-element.149, f32[3072]{0:T(1024)S(1)} %convert_element_type.260, f32[512,3072]{1,0:T(8,128)} %fusion.109, ...), kind=kOutput, calls=%fused_computation.35 | convolution fusion | flops 2469390336 | bytes 43290624 | tf_op jit(solution)/shard_map/td,fd->tf/dot_general | solution.py:182
  494.7 22.6 %convolution_convert_fusion.1 = bf16[12,64,2048]{2,1,0:T(8,128)(2,1)} fusion(bf16[512,12,64]{0,2,1:T(8,128)(2,1)S(1)} %bitcast.213, f32[12,512,2048]{2,1,0:T(8,128)} %get-tuple-element.142, f32[12,512]{1,0:T(8,128)S(1)} %log_add_fusion.1, pred[512,2048]{1,0:T(8,128)(4,1)S(1)} %broadcast_compare_fusion.1), kind=kOutput, calls=%fused_computation.71 | convolution fusion | flops 1662517248 | bytes 55336960 | tf_op jit(solution)/shard_map/hqk,qhd->khd/dot_general | solution.py:222
  525.3 22.9 %convolution_convert_fusion = bf16[12,64,2048]{2,1,0:T(8,128)(2,1)} fusion(bf16[512,12,64]{0,2,1:T(8,128)(2,1)S(1)} %bitcast.211, f32[12,512,2048]{2,1,0:T(8,128)} %get-tuple-element.146, f32[12,512]{1,0:T(8,128)S(1)} %copy-done.52, pred[512,2048]{1,0:T(8,128)(4,1)S(1)} %copy-done.1), kind=kOutput, calls=%fused_computation.70 | convolution fusion | flops 1662517248 | bytes 55336960 | tf_op jit(solution)/shard_map/hqk,qhd->khd/dot_general | solution.py:222
  549.4 37.9 %multiply_reduce_fusion.1 = (f32[12,512]{1,0:T(8,128)S(1)}, f32[12,512,2048]{2,1,0:T(8,128)}) fusion(f32[12,512,2048]{2,1,0:T(8,128)} %get-tuple-element.142, f32[12,512]{1,0:T(8,128)S(1)} %log_add_fusion.1, pred[512,2048]{1,0:T(8,128)(4,1)S(1)} %broadcast_compare_fusion.1, bf16[512,12,64]{0,2,1:T(8,128)(2,1)S(1)} %bitcast.214, ...), kind=kOutput, calls=%fused_computation.3 | convolution fusion | flops 1673521152 | bytes 105693184 | tf_op jit(solution)/shard_map/qhd,khd->hqk/dot_general | solution.py:204
  587.3 40.5 %multiply_convert_fusion.1 = bf16[12,512,2048]{2,1,0:T(8,128)(2,1)} fusion(f32[12,512,2048]{2,1,0:T(8,128)} %get-tuple-element.158, f32[12,512,2048]{2,1,0:T(8,128)} %get-tuple-element.142, f32[12,512]{1,0:T(8,128)S(1)} %get-tuple-element.157, f32[12,512]{1,0:T(8,128)S(1)} %log_add_fusion.1, pred[512,2048]{1,0:T(8,128)(4,1)S(1)} %broadcast_compare_fusion.1), kind=kLoop, calls=%fused_computation.2 | loop fusion | flops 75497472 | bytes 126926848 | tf_op jit(solution)/shard_map/convert_element_type | solution.py:208
  643.2 38.8 %multiply_reduce_fusion = (f32[12,512]{1,0:T(8,128)S(1)}, f32[12,512,2048]{2,1,0:T(8,128)}) fusion(f32[12,512,2048]{2,1,0:T(8,128)} %get-tuple-element.146, f32[12,512]{1,0:T(8,128)S(1)} %copy-done.52, pred[512,2048]{1,0:T(8,128)(4,1)S(1)} %copy-done.1, bf16[512,12,64]{0,2,1:T(8,128)(2,1)S(1)} %bitcast.212, bf16[2048,12,64]{0,2,1:T(8,128)(2,1)} %bitcast.198), kind=kOutput, calls=%fused_computation.1 | convolution fusion | flops 1673521152 | bytes 105693184 | tf_op jit(solution)/shard_map/qhd,khd->hqk/dot_general | solution.py:204
  682.0 40.4 %multiply_convert_fusion = bf16[12,512,2048]{2,1,0:T(8,128)(2,1)} fusion(f32[12,512,2048]{2,1,0:T(8,128)} %get-tuple-element.156, f32[12,512,2048]{2,1,0:T(8,128)} %get-tuple-element.146, f32[12,512]{1,0:T(8,128)S(1)} %get-tuple-element.155, f32[12,512]{1,0:T(8,128)S(1)} %copy-done.52, pred[512,2048]{1,0:T(8,128)(4,1)S(1)} %copy-done.1), kind=kLoop, calls=%fused_computation | loop fusion | flops 75497472 | bytes 126926848 | tf_op jit(solution)/shard_map/convert_element_type | solution.py:208
  722.4 14.3 multiply_convert_fusion.2
  832.7 40.3 %all-reduce.18 = (f32[768]{0:T(1024)S(1)}, f32[768]{0:T(1024)S(1)}, f32[768]{0:T(1024)S(1)}, f32[768]{0:T(1024)S(1)}, f32[768]{0:T(1024)S(1)}, /*index=5*/f32[30...) all-reduce(f32[768]{0:T(1024)S(1)} %add.341, ...), channel_id=7, replica_groups=mesh['dp'=8,'ctx'=4] {'dp','ctx'}, use_global_device_ids=true, to_apply=%region_29.31.clone | all-reduce | flops 9216 | bytes 73728
  886.1 96.9 %reduce-scatter.31.cloned.1.call-done = f32[24,768]{1,0:T(8,128)} async-done(((f32[768,768]{1,0:T(8,128)}), f32[24,768]{1,0:T(8,128)}) %reduce-scatter.31.cloned.1.call-update) | async-done | bytes 73744
  983.0 104.4 %reduce-scatter.35.cloned.1.call-done = f32[24,768]{1,0:T(8,128)} async-done(((f32[768,768]{1,0:T(8,128)}), f32[24,768]{1,0:T(8,128)}) %reduce-scatter.35.cloned.1.call-update) | async-done | bytes 73744
  1087.3 104.4 %reduce-scatter.33.cloned.1.call-done = f32[24,768]{1,0:T(8,128)} async-done(((f32[768,768]{1,0:T(8,128)}), f32[24,768]{1,0:T(8,128)}) %reduce-scatter.33.cloned.1.call-update) | async-done | bytes 73744
  1191.7 141.5 %reduce-scatter.27.cloned.1.call-done = f32[24,3072]{1,0:T(8,128)} async-done(((f32[768,3072]{1,0:T(8,128)}), f32[24,3072]{1,0:T(8,128)}) %reduce-scatter.27.cloned.1.call-update) | async-done | bytes 294928 | tf_op jit(solution)/shard_map/reduce_scatter | solution.py:272
  1333.2 141.5 %reduce-scatter.29.cloned.1.call-done = f32[96,768]{1,0:T(8,128)} async-done(((f32[3072,768]{1,0:T(8,128)}), f32[96,768]{1,0:T(8,128)}) %reduce-scatter.29.cloned.1.call-update) | async-done | bytes 294928 | tf_op jit(solution)/shard_map/reduce_scatter | solution.py:272
  (381 shorter events, 313.3 us)
Async XLA Ops:
  7.2 60.8 %all-gather.9.cloned.1.call-start = ((), (), s32[]{:S(2)}) async-start(), calls=%async_computation.10 | async-start | bytes 1216512 | tf_op jit(solution)/shard_map/all_gather | solution.py:41
  7.9 115.8 %all-gather.15.cloned.1.call-start = ((), (), s32[]{:S(2)}) async-start(), calls=%async_computation.13 | async-start | bytes 1216512 | tf_op jit(solution)/shard_map/all_gather | solution.py:40
  8.7 172.3 %all-gather.13.cloned.1.call-start = ((), (), s32[]{:S(2)}) async-start(), calls=%async_computation.12 | async-start | bytes 1216512 | tf_op jit(solution)/shard_map/all_gather | solution.py:38
  9.4 313.0 %all-gather.23.cloned.1.call-start = ((), (), s32[]{:S(2)}) async-start(), calls=%async_computation.17 | async-start | bytes 3932160 | tf_op jit(solution)/shard_map/all_gather | solution.py:130
  71.3 276.4 %all-gather.17.cloned.1.call-start = ((), (), s32[]{:S(2)}) async-start(), calls=%async_computation.14 | async-start | bytes 1216512 | tf_op jit(solution)/shard_map/all_gather | solution.py:43
  71.9 279.6 %all-gather.11.cloned.1.call-start = ((), (), s32[]{:S(2)}) async-start(), calls=%async_computation.11 | async-start | bytes 3932160 | tf_op jit(solution)/shard_map/all_gather | solution.py:130
  73.7 306.0 %all-gather.19.cloned.1.call-start = ((), (), s32[]{:S(2)}) async-start(), calls=%async_computation.15 | async-start | bytes 4866048 | tf_op jit(solution)/shard_map/all_gather | solution.py:47
  74.4 361.0 %all-gather.21.cloned.1.call-start = ((), (), s32[]{:S(2)}) async-start(), calls=%async_computation.16 | async-start | bytes 4866048 | tf_op jit(solution)/shard_map/all_gather | solution.py:49
  75.2 706.6 %reduce-scatter.19.cloned.1.call-start = ((), (), s32[]{:S(2)}) async-start(), calls=%async_computation.19 | async-start | bytes 3932160 | tf_op jit(solution)/shard_map/reduce_scatter | solution.py:229
  126.8 17.9 %collective-permute-start = (bf16[512,768]{1,0:T(8,128)(2,1)}, bf16[512,768]{1,0:T(8,128)(2,1)}, u32[]{:S(2)}, u32[]{:S(2)}) collective-permute-start(bf16[512,768]{1,0:T(8,128)(2,1)} %convolution_convert_fusion.7), channel_id=1, source_target_pairs={{0,1},{1,2},{2,3},{3,0},{4,5},{5,6},{6,7},{7,4},{8,9},{9,10},{10,1... | collective-permute-start | bytes 2359304 | tf_op jit(solution)/shard_map/ppermute | solution.py:18
  127.7 64.1 %collective-permute-start.2 = (bf16[512,768]{1,0:T(8,128)(2,1)}, bf16[512,768]{1,0:T(8,128)(2,1)}, u32[]{:S(2)}, u32[]{:S(2)}) collective-permute-start(bf16[512,768]{1,0:T(8,128)(2,1)} %convolution_convert_fusion.7), channel_id=1, source_target_pairs={{0,3},{1,0},{2,1},{3,2},{4,7},{5,4},{6,5},{7,6},{8,11},{9,8},{10,9... | collective-permute-start | bytes 2359304 | tf_op jit(solution)/shard_map/ppermute | solution.py:20
  132.1 59.4 %collective-permute-start.3 = (bf16[512,768]{1,0:T(8,128)(2,1)}, bf16[512,768]{1,0:T(8,128)(2,1)}, u32[]{:S(2)}, u32[]{:S(2)}) collective-permute-start(bf16[512,768]{1,0:T(8,128)(2,1)} %convolution_convert_fusion.6), channel_id=1, source_target_pairs={{0,1},{1,2},{2,3},{3,0},{4,5},{5,6},{6,7},{7,4},{8,9},{9,10},{10,1... | collective-permute-start | bytes 2359304 | tf_op jit(solution)/shard_map/ppermute | solution.py:18
  144.7 47.1 %collective-permute-start.1 = (bf16[512,768]{1,0:T(8,128)(2,1)}, bf16[512,768]{1,0:T(8,128)(2,1)}, u32[]{:S(2)}, u32[]{:S(2)}) collective-permute-start(bf16[512,768]{1,0:T(8,128)(2,1)} %collective-permute-done), channel_id=1, source_target_pairs={{0,1},{1,2},{2,3},{3,0},{4,5},{5,6},{6,7},{7,4},{8,9},{9,10},{10,1... | collective-permute-start | bytes 2359304 | tf_op jit(solution)/shard_map/ppermute | solution.py:18
  147.4 60.0 %collective-permute-start.5 = (bf16[512,768]{1,0:T(8,128)(2,1)}, bf16[512,768]{1,0:T(8,128)(2,1)}, u32[]{:S(2)}, u32[]{:S(2)}) collective-permute-start(bf16[512,768]{1,0:T(8,128)(2,1)} %convolution_convert_fusion.6), channel_id=1, source_target_pairs={{0,3},{1,0},{2,1},{3,2},{4,7},{5,4},{6,5},{7,6},{8,11},{9,8},{10,9... | collective-permute-start | bytes 2359304 | tf_op jit(solution)/shard_map/ppermute | solution.py:20
  191.4 26.0 %collective-permute-start.4 = (bf16[512,768]{1,0:T(8,128)(2,1)}, bf16[512,768]{1,0:T(8,128)(2,1)}, u32[]{:S(2)}, u32[]{:S(2)}) collective-permute-start(bf16[512,768]{1,0:T(8,128)(2,1)} %collective-permute-done.3), channel_id=1, source_target_pairs={{0,1},{1,2},{2,3},{3,0},{4,5},{5,6},{6,7},{7,4},{8,9},{9,10},{10,1... | collective-permute-start | bytes 2359304 | tf_op jit(solution)/shard_map/ppermute | solution.py:18
  517.3 267.8 %reduce-scatter.23.cloned.1.call-start = ((), (), s32[]{:S(2)}) async-start(), calls=%async_computation.21 | async-start | bytes 3932160 | tf_op jit(solution)/shard_map/reduce_scatter | solution.py:229
  548.3 244.2 %reduce-scatter.17.cloned.1.call-start = ((), (), s32[]{:S(2)}) async-start(), calls=%async_computation.18 | async-start | bytes 3932160 | tf_op jit(solution)/shard_map/reduce_scatter | solution.py:226
  642.1 153.7 %reduce-scatter.21.cloned.1.call-start = ((), (), s32[]{:S(2)}) async-start(), calls=%async_computation.20 | async-start | bytes 3932160 | tf_op jit(solution)/shard_map/reduce_scatter | solution.py:226
  736.7 149.3 %reduce-scatter.25.cloned.1.call-start = ((), (), s32[]{:S(2)}) async-start(), calls=%async_computation.22 | async-start | bytes 2433024 | tf_op jit(solution)/shard_map/reduce_scatter | solution.py:272
  742.7 240.3 %reduce-scatter.31.cloned.1.call-start = ((), (), s32[]{:S(2)}) async-start(), calls=%async_computation.25 | async-start | bytes 2433024
  781.7 305.6 %reduce-scatter.35.cloned.1.call-start = ((), (), s32[]{:S(2)}) async-start(), calls=%async_computation.27 | async-start | bytes 2433024
  792.4 399.3 %reduce-scatter.33.cloned.1.call-start = ((), (), s32[]{:S(2)}) async-start(), calls=%async_computation.26 | async-start | bytes 2433024
  803.2 530.0 %reduce-scatter.27.cloned.1.call-start = ((), (), s32[]{:S(2)}) async-start(), calls=%async_computation.23 | async-start | bytes 9732096 | tf_op jit(solution)/shard_map/reduce_scatter | solution.py:272
  814.4 660.2 %reduce-scatter.29.cloned.1.call-start = ((), (), s32[]{:S(2)}) async-start(), calls=%async_computation.24 | async-start | bytes 9732096 | tf_op jit(solution)/shard_map/reduce_scatter | solution.py:272
  (94 other events, 1955.7 us)
Sparse Core Ops, SparseCore 0:
  10.9 57.0 all-gather.8
  70.9 52.7 all-gather.14
  126.6 54.3 all-gather.12
  183.0 34.5 all-gather.22
  220.3 54.8 all-gather.16
  276.7 27.4 all-gather.10
  307.1 63.4 all-gather.18
  373.5 61.9 all-gather.20
  517.4 36.0 reduce-scatter.18
  555.9 37.7 reduce-scatter.22
  642.2 36.9 reduce-scatter.16
  736.9 36.0 reduce-scatter.20
  778.8 99.6 reduce-scatter.24
  884.3 98.6 reduce-scatter.30
  988.7 98.6 reduce-scatter.34
  1093.0 98.6 reduce-scatter.32
  1198.0 135.1 reduce-scatter.26
  1339.5 135.0 reduce-scatter.28
